TPU v7x, 32 devices: a whole 2x2x4 slice. The times are simulated.
32 devices in a mesh: seq: 8 (over y, x, core), head: 4 (over z).
Axes of the slice: x: 2, y: 2, z: 4, core: 2. Of those that a mesh axis runs over, the one named last changes fastest.
Arguments:
- tokens: bfloat16 [24576, 768], P(('seq', 'head')), may hold values from -6 to 6
- cotangent: bfloat16 [24576, 768], P(('seq', 'head')), may hold values from -6 to 6
- lengths: int32 [8, 24], P('seq'), may hold values from 1 to 512, 3072 in all within a row
- labels: int32 [8, 24], P('seq'), may hold values from 0 to 2
- w_qkv: bfloat16 [768, 2304], replicated, may hold values from -0.3125 to 0.3125
- b_query: float32 [768], replicated, may hold values from -3 to 3
- b_value: float32 [768], replicated, may hold values from -3 to 3
- w_out: bfloat16 [768, 768], replicated, may hold values from -0.625 to 0.625
- b_out: float32 [768], replicated, may hold values from -3 to 3
- gain_attn: float32 [768], replicated, may hold values from 0.1 to 1.9
- shift_attn: float32 [768], replicated, may hold values from -3 to 3
- w_in: bfloat16 [768, 3072], replicated, may hold values from -0.21875 to 0.21875
- b_in: float32 [3072], replicated, may hold values from -3 to 3
- w_back: bfloat16 [3072, 768], replicated, may hold values from -0.15625 to 0.15625
- b_back: float32 [768], replicated, may hold values from -3 to 3
- gain_ffn: float32 [768], replicated, may hold values from 0.1 to 1.9
- shift_ffn: float32 [768], replicated, may hold values from -3 to 3
- w_pool: bfloat16 [768, 768], replicated, may hold values from -0.21875 to 0.21875
- b_pool: float32 [768], replicated, may hold values from -3 to 3
- w_class: float32 [768, 3], replicated, may hold values from -0.625 to 0.625
Outputs:
- output: bfloat16 [24576, 768], P(('seq', 'head'))
- grad_tokens: float32 [24576, 768], P(('seq', 'head'))
- grad_w_qkv: float32 [768, 2304], P(('seq', 'head'))
- grad_b_query: float32 [768], P(('seq', 'head'))
- grad_b_value: float32 [768], P(('seq', 'head'))
- grad_w_out: float32 [768, 768], P(('seq', 'head'))
- grad_b_out: float32 [768], P(('seq', 'head'))
- grad_gain_attn: float32 [768], P(('seq', 'head'))
- grad_shift_attn: float32 [768], P(('seq', 'head'))
- grad_w_in: float32 [768, 3072], P(('seq', 'head'))
- grad_b_in: float32 [3072], P(('seq', 'head'))
- grad_w_back: float32 [3072, 768], P(('seq', 'head'))
- grad_b_back: float32 [768], P(('seq', 'head'))
- grad_gain_ffn: float32 [768], P(('seq', 'head'))
- grad_shift_ffn: float32 [768], P(('seq', 'head'))
- grad_w_pool: float32 [768, 768], P(('seq', 'head'))
- grad_b_pool: float32 [768], P(('seq', 'head'))
- grad_w_class: float32 [768, 3], P(('seq', 'head'))
- entropy: float32 [], replicated
Inputs may be any that keep to these rules, and one draw needn't show every extreme that they name: Each row of 24 lengths sums to 3072, and its largest length is 512.
All inputs are finite; a program needn't handle non-finite values.
Results may differ from a plain program's by a relative error of at most 0.014.
The roundings to bfloat16 on the way count: a program that leaves them out, or rounds other values in their place, can miss the bound.
Values may be sent and summed in bfloat16 or wider, within the bound.
A program may use at most 192 MiB of HBM per device.

v0:
```python
import jax
import jax.numpy as jnp
from jax import lax
from jax.sharding import PartitionSpec as P

HEAD_DIM = 64
MAXLEN = 512
eps = 1e-05
big_neg = -1e30
highest = lax.Precision.HIGHEST


def exact_gelu(values):
    return jax.nn.gelu(values, approximate=False)


def layer_norm(hidden, gain_vec, shift_vec):
    centred = hidden - jnp.mean(hidden, axis=-1, keepdims=True)
    inv_std = lax.rsqrt(jnp.mean(centred * centred, axis=-1, keepdims=True) + eps)
    normed = centred * inv_std
    return (normed * gain_vec + shift_vec, normed, inv_std)


def norm_back(grad_out, normed, inv_std, gain_vec):
    grad_norm = grad_out * gain_vec
    inner = grad_norm - jnp.mean(grad_norm, axis=-1, keepdims=True)
    inner = inner - normed * jnp.mean(grad_norm * normed, axis=-1, keepdims=True)
    return (inv_std * inner, jnp.sum(grad_out * normed, axis=0), jnp.sum(grad_out, axis=0))


def block_scores(q_block, k_window, seg_query, seg_key):
    raw_scores = jnp.einsum(
        "hdq,hdk->hqk", q_block, k_window, preferred_element_type=jnp.float32
    ) * HEAD_DIM ** (-0.5)
    same_seq = seg_query[:, None] == seg_key[None, :]
    return jnp.where(same_seq[None], raw_scores, big_neg)


def pad_keys(k_heads, v_heads, seg_all, block_len):
    padding = ((0, 0), (0, 0), (block_len, block_len))
    return (
        jnp.pad(k_heads, padding),
        jnp.pad(v_heads, padding),
        jnp.pad(seg_all, (block_len, block_len), constant_values=-1),
    )


def attend_forward(q_heads, k_heads, v_heads, seg_all, block_len):
    local_heads, head_width, group_rows = q_heads.shape
    k_padded, v_padded, seg_padded = pad_keys(k_heads, v_heads, seg_all, block_len)

    def one_block(block_index):
        offset = block_index * block_len
        q_block = lax.dynamic_slice_in_dim(q_heads, offset, block_len, 2)
        k_window = lax.dynamic_slice_in_dim(k_padded, offset, 3 * block_len, 2)
        v_window = lax.dynamic_slice_in_dim(v_padded, offset, 3 * block_len, 2)
        seg_query = lax.dynamic_slice_in_dim(seg_all, offset, block_len, 0)
        seg_key = lax.dynamic_slice_in_dim(seg_padded, offset, 3 * block_len, 0)
        scores = block_scores(q_block, k_window, seg_query, seg_key)
        row_peak = jnp.max(scores, axis=-1, keepdims=True)
        expo = jnp.exp(scores - row_peak)
        row_total = jnp.sum(expo, axis=-1, keepdims=True)
        weights_low = (expo / row_total).astype(jnp.bfloat16)
        context_block = jnp.einsum(
            "hdk,hqk->hdq", v_window, weights_low, preferred_element_type=jnp.float32
        )
        return (context_block, (row_peak + jnp.log(row_total))[..., 0])

    context_blocks, log_norm = lax.map(
        one_block, jnp.arange(group_rows // block_len, dtype=jnp.int32)
    )
    context = jnp.transpose(context_blocks, (1, 2, 0, 3)).reshape(
        local_heads * head_width, group_rows
    )
    return (context, log_norm)


def attend_backward(q_heads, k_heads, v_heads, grad_ctx, seg_all, log_norm, block_len):
    local_heads, head_width, group_rows = q_heads.shape
    k_padded, v_padded, seg_padded = pad_keys(k_heads, v_heads, seg_all, block_len)

    def one_block(carry, inputs):
        grad_keys, grad_values = carry
        block_index, block_norm = inputs
        offset = block_index * block_len
        q_block = lax.dynamic_slice_in_dim(q_heads, offset, block_len, 2)
        k_window = lax.dynamic_slice_in_dim(k_padded, offset, 3 * block_len, 2)
        v_window = lax.dynamic_slice_in_dim(v_padded, offset, 3 * block_len, 2)
        grad_block = lax.dynamic_slice_in_dim(grad_ctx, offset, block_len, 2)
        seg_query = lax.dynamic_slice_in_dim(seg_all, offset, block_len, 0)
        seg_key = lax.dynamic_slice_in_dim(seg_padded, offset, 3 * block_len, 0)
        scores = block_scores(q_block, k_window, seg_query, seg_key)
        weights = jnp.exp(scores - block_norm[..., None])
        weights_low = weights.astype(jnp.bfloat16)
        grad_weights = jnp.einsum(
            "hdq,hdk->hqk", grad_block, v_window, preferred_element_type=jnp.float32
        )
        row_dot = jnp.sum(weights * grad_weights, axis=-1, keepdims=True)
        grad_scores = (weights * (grad_weights - row_dot) * HEAD_DIM ** (-0.5)).astype(jnp.bfloat16)
        grad_query = jnp.einsum(
            "hqk,hdk->hdq", grad_scores, k_window, preferred_element_type=jnp.float32
        )
        key_part = jnp.einsum(
            "hqk,hdq->hdk", grad_scores, q_block, preferred_element_type=jnp.float32
        )
        value_part = jnp.einsum(
            "hqk,hdq->hdk", weights_low, grad_block, preferred_element_type=jnp.float32
        )
        grad_keys = lax.dynamic_update_slice_in_dim(
            grad_keys,
            lax.dynamic_slice_in_dim(grad_keys, offset, 3 * block_len, 2) + key_part,
            offset,
            2,
        )
        grad_values = lax.dynamic_update_slice_in_dim(
            grad_values,
            lax.dynamic_slice_in_dim(grad_values, offset, 3 * block_len, 2) + value_part,
            offset,
            2,
        )
        return ((grad_keys, grad_values), grad_query)

    zero_pad = jnp.zeros(k_padded.shape, jnp.float32)
    block_ids = jnp.arange(group_rows // block_len, dtype=jnp.int32)
    (grad_keys, grad_values), grad_queries = lax.scan(
        one_block, (zero_pad, zero_pad), (block_ids, log_norm)
    )
    grad_q = jnp.transpose(grad_queries, (1, 2, 0, 3)).reshape(local_heads * head_width, group_rows)
    grad_k = grad_keys[:, :, block_len : block_len + group_rows].reshape(
        local_heads * head_width, group_rows
    )
    grad_v = grad_values[:, :, block_len : block_len + group_rows].reshape(
        local_heads * head_width, group_rows
    )
    return (grad_q, grad_k, grad_v)


def local(
    tokens,
    cotangent,
    lengths,
    labels,
    w_qkv,
    b_query,
    b_value,
    w_out,
    b_out,
    gain_attn,
    shift_attn,
    w_in,
    b_in,
    w_back,
    b_back,
    gain_ffn,
    shift_ffn,
    w_pool,
    b_pool,
    w_class,
):
    n_head = lax.axis_size("head")
    n_seq = lax.axis_size("seq")
    head_index = lax.axis_index("head")
    tok_rows, model_width = tokens.shape
    group_rows = tok_rows * n_head
    block_len = MAXLEN
    local_width = model_width // n_head
    local_heads = local_width // HEAD_DIM
    contract_first = (((0,), (0,)), ((), ()))
    contract_last = (((1,), (1,)), ((), ()))
    seq_lengths = lengths[0]
    starts = jnp.cumsum(seq_lengths) - seq_lengths
    group_pos = jnp.arange(group_rows, dtype=jnp.int32)
    seg_all = jnp.sum((starts[None, :] <= group_pos[:, None]).astype(jnp.int32), axis=1) - 1
    qkv_cols = lax.dot_general(
        w_qkv, tokens, (((0,), (1,)), ((), ())), preferred_element_type=jnp.float32
    )
    bias_cols = jnp.concatenate([b_query, jnp.zeros_like(b_query), b_value])[:, None]
    qkv_low = (qkv_cols + bias_cols).astype(jnp.bfloat16).reshape(3, model_width, tok_rows)
    qkv_heads = lax.all_to_all(qkv_low, "head", split_axis=1, concat_axis=2, tiled=True)
    q_heads = qkv_heads[0].reshape(local_heads, HEAD_DIM, group_rows)
    k_heads = qkv_heads[1].reshape(local_heads, HEAD_DIM, group_rows)
    v_heads = qkv_heads[2].reshape(local_heads, HEAD_DIM, group_rows)
    context, log_norm = attend_forward(q_heads, k_heads, v_heads, seg_all, block_len)
    context_cols = lax.all_to_all(
        context.astype(jnp.bfloat16), "head", split_axis=1, concat_axis=0, tiled=True
    )
    attn_out = (
        lax.dot_general(context_cols, w_out, contract_first, preferred_element_type=jnp.float32)
        + b_out
    )
    normed_attn, unit_attn, inv_attn = layer_norm(
        tokens.astype(jnp.float32) + attn_out, gain_attn, shift_attn
    )
    middle = normed_attn.astype(jnp.bfloat16)
    pre_act = jnp.dot(middle, w_in, preferred_element_type=jnp.float32) + b_in
    activated_f32, gelu_pull = jax.vjp(exact_gelu, pre_act)
    activated = activated_f32.astype(jnp.bfloat16)
    ffn_out = jnp.dot(activated, w_back, preferred_element_type=jnp.float32) + b_back
    normed_ffn, unit_ffn, inv_ffn = layer_norm(
        middle.astype(jnp.float32) + ffn_out, gain_ffn, shift_ffn
    )
    output = normed_ffn.astype(jnp.bfloat16)
    row_base = head_index * tok_rows
    my_rows = row_base + jnp.arange(tok_rows, dtype=jnp.int32)
    my_seg = lax.dynamic_slice_in_dim(seg_all, row_base, tok_rows, 0)
    is_start = jnp.take(starts, my_seg) == my_rows
    owner_sel = (starts[:, None] == my_rows[None, :]).astype(jnp.bfloat16)
    owned = jnp.sum(owner_sel.astype(jnp.float32), axis=1)
    cls_low = jnp.dot(owner_sel, output, preferred_element_type=jnp.float32).astype(jnp.bfloat16)
    pooled = jnp.tanh(jnp.dot(cls_low, w_pool, preferred_element_type=jnp.float32) + b_pool)
    logits = jnp.dot(pooled, w_class, precision=highest)
    class_peak = jnp.max(logits, axis=-1, keepdims=True)
    class_exp = jnp.exp(logits - class_peak)
    class_total = jnp.sum(class_exp, axis=-1, keepdims=True)
    class_probs = class_exp / class_total
    ramp_norm = (class_peak + jnp.log(class_total))[:, 0]
    entropy_terms = owned * (ramp_norm - jnp.sum(class_probs * logits, axis=-1))
    entropy_all = lax.psum(jnp.sum(entropy_terms), ("seq", "head"))
    entropy_mean = entropy_all / (n_seq * labels.shape[1])
    onehot = (labels[0][:, None] == jnp.arange(w_class.shape[1], dtype=jnp.int32)[None, :]).astype(
        jnp.float32
    )
    grad_logits = (class_probs - onehot) * owned[:, None]
    grad_class = lax.dot_general(pooled, grad_logits, contract_first, precision=highest)
    grad_pooled = lax.dot_general(grad_logits, w_class, contract_last, precision=highest)
    grad_pre_pool = (grad_pooled * (1.0 - pooled * pooled)).astype(jnp.bfloat16)
    grad_pool = lax.dot_general(
        cls_low, grad_pre_pool, contract_first, preferred_element_type=jnp.float32
    )
    grad_bpool = jnp.sum(grad_pre_pool.astype(jnp.float32), axis=0)
    grad_cls = lax.dot_general(
        grad_pre_pool, w_pool, contract_last, preferred_element_type=jnp.float32
    )
    cls_back = jnp.where(is_start[:, None], jnp.take(grad_cls, my_seg, axis=0), 0.0)
    grad_result = cotangent.astype(jnp.float32) + cls_back
    grad_ffn_res, grad_gain_ffn, grad_shift_ffn = norm_back(
        grad_result, unit_ffn, inv_ffn, gain_ffn
    )
    grad_ffn = grad_ffn_res.astype(jnp.bfloat16)
    grad_wback = lax.dot_general(
        activated, grad_ffn, contract_first, preferred_element_type=jnp.float32
    )
    grad_bback = jnp.sum(grad_ffn.astype(jnp.float32), axis=0)
    grad_act = lax.dot_general(grad_ffn, w_back, contract_last, preferred_element_type=jnp.float32)
    grad_pre = gelu_pull(grad_act)[0].astype(jnp.bfloat16)
    grad_win = lax.dot_general(middle, grad_pre, contract_first, preferred_element_type=jnp.float32)
    grad_bin = jnp.sum(grad_pre.astype(jnp.float32), axis=0)
    grad_middle = grad_ffn_res + lax.dot_general(
        grad_pre, w_in, contract_last, preferred_element_type=jnp.float32
    )
    grad_attn_res, grad_gain_attn, grad_shift_attn = norm_back(
        grad_middle, unit_attn, inv_attn, gain_attn
    )
    grad_attn = grad_attn_res.astype(jnp.bfloat16)
    grad_wout = lax.dot_general(
        context_cols, grad_attn, (((1,), (0,)), ((), ())), preferred_element_type=jnp.float32
    )
    grad_bout = jnp.sum(grad_attn.astype(jnp.float32), axis=0)
    grad_ctx_cols = lax.dot_general(
        w_out, grad_attn, contract_last, preferred_element_type=jnp.float32
    )
    grad_ctx_heads = lax.all_to_all(
        grad_ctx_cols.astype(jnp.bfloat16), "head", split_axis=0, concat_axis=1, tiled=True
    )
    grad_q, grad_k, grad_v = attend_backward(
        q_heads,
        k_heads,
        v_heads,
        grad_ctx_heads.reshape(local_heads, HEAD_DIM, group_rows),
        seg_all,
        log_norm,
        block_len,
    )
    grad_stack = jnp.stack([grad_q, grad_k, grad_v]).astype(jnp.bfloat16)
    grad_qkv = lax.all_to_all(grad_stack, "head", split_axis=2, concat_axis=1, tiled=True).reshape(
        3 * model_width, tok_rows
    )
    grad_tokens = grad_attn_res + lax.dot_general(
        grad_qkv, w_qkv, (((0,), (1,)), ((), ())), preferred_element_type=jnp.float32
    )
    grad_wqkv = lax.dot_general(
        tokens, grad_qkv, (((0,), (1,)), ((), ())), preferred_element_type=jnp.float32
    )
    grad_bquery = jnp.sum(grad_qkv[:model_width].astype(jnp.float32), axis=1)
    grad_bvalue = jnp.sum(grad_qkv[2 * model_width :].astype(jnp.float32), axis=1)
    summed = (
        lax.psum_scatter(grad_wqkv, ("seq", "head"), scatter_dimension=0, tiled=True),
        lax.psum_scatter(grad_bquery, ("seq", "head"), scatter_dimension=0, tiled=True),
        lax.psum_scatter(grad_bvalue, ("seq", "head"), scatter_dimension=0, tiled=True),
        lax.psum_scatter(grad_wout, ("seq", "head"), scatter_dimension=0, tiled=True),
        lax.psum_scatter(grad_bout, ("seq", "head"), scatter_dimension=0, tiled=True),
        lax.psum_scatter(grad_gain_attn, ("seq", "head"), scatter_dimension=0, tiled=True),
        lax.psum_scatter(grad_shift_attn, ("seq", "head"), scatter_dimension=0, tiled=True),
        lax.psum_scatter(grad_win, ("seq", "head"), scatter_dimension=0, tiled=True),
        lax.psum_scatter(grad_bin, ("seq", "head"), scatter_dimension=0, tiled=True),
        lax.psum_scatter(grad_wback, ("seq", "head"), scatter_dimension=0, tiled=True),
        lax.psum_scatter(grad_bback, ("seq", "head"), scatter_dimension=0, tiled=True),
        lax.psum_scatter(grad_gain_ffn, ("seq", "head"), scatter_dimension=0, tiled=True),
        lax.psum_scatter(grad_shift_ffn, ("seq", "head"), scatter_dimension=0, tiled=True),
        lax.psum_scatter(grad_pool, ("seq", "head"), scatter_dimension=0, tiled=True),
        lax.psum_scatter(grad_bpool, ("seq", "head"), scatter_dimension=0, tiled=True),
        lax.psum_scatter(grad_class, ("seq", "head"), scatter_dimension=0, tiled=True),
    )
    return (
        output,
        grad_tokens,
        summed[0],
        summed[1],
        summed[2],
        summed[3],
        summed[4],
        summed[5],
        summed[6],
        summed[7],
        summed[8],
        summed[9],
        summed[10],
        summed[11],
        summed[12],
        summed[13],
        summed[14],
        summed[15],
        entropy_mean,
    )


def solution(mesh):
    placed = (
        P(("seq", "head"), None),
        P(("seq", "head"), None),
        P("seq", None),
        P("seq", None),
        P(),
        P(),
        P(),
        P(),
        P(),
        P(),
        P(),
        P(),
        P(),
        P(),
        P(),
        P(),
        P(),
        P(),
        P(),
        P(),
    )
    return jax.shard_map(
        local,
        mesh=mesh,
        in_specs=placed,
        out_specs=(
            P(("seq", "head"), None),
            P(("seq", "head"), None),
            P(("seq", "head"), None),
            P(("seq", "head")),
            P(("seq", "head")),
            P(("seq", "head"), None),
            P(("seq", "head")),
            P(("seq", "head")),
            P(("seq", "head")),
            P(("seq", "head"), None),
            P(("seq", "head")),
            P(("seq", "head"), None),
            P(("seq", "head")),
            P(("seq", "head")),
            P(("seq", "head")),
            P(("seq", "head"), None),
            P(("seq", "head")),
            P(("seq", "head"), None),
            P(),
        ),
        check_vma=False,
    )
```

profile of v0, /device:TPU:0, one launch (start us, length us, event | category | flops | bytes accessed | tf_op | source)
XLA Modules:
  0.0 1120.1 jit_solution(16411158388768672741)
XLA Ops:
  29.1 101.8 %all-to-all-done = bf16[3,768,768]{2,0,1:T(4,128)(2,1)} async-done(((bf16[3,768,768]{2,0,1:T(4,128)(2,1)}), bf16[3,768,768]{2,0,1:T(4,128)(2,1)}, u32[]{:S(2)}, u32[]{:S(2)}) %all-to-all-start) | async-done | bytes 3538976 | tf_op jit(solution)/shard_map/all_to_all | solution.py:179
  130.9 11.1 fusion.92
  167.8 88.9 %while.26 = (s32[]{:T(128)}, bf16[6,3,64,512]{3,2,1,0:T(8,128)(2,1)}, f32[6,3,512]{2,1,0:T(4,128)}, s32[6]{0:T(128)S(1)}, bf16[3,64,4096]{2,1,0:T(8,128)(2,1)}, ...) while((s32[]{:T(128)}, ...), condition=%wide.region_5.6_spmd, body=%wide.region_2.5_spmd.sunk | while | flops 633076224 | bytes 33304036 | solution.py:69
  276.5 16.7 %fusion.71 = (pred[768]{0:T(1024)(128)(4,1)}, s32[768]{0:T(1024)S(1)}) fusion(s32[]{:T(128)} %bitcast.16, s32[]{:T(128)} %bitcast.17, s32[]{:T(128)} %bitcast.18, s32[]{:T(128)} %bitcast.19, s32[]{:T(128)} %bitcast.20, s32[]{:T(128)} %bitcast.21, s32[]{:T(128)} %bitcast.22, s32[]{:T(128)} %bitcast.23, s32[]{:T(128)} %bitcast.24, s32[]{:T(128)} %bitcast.25, ...), kind=kLoop, calls=%fused_computation.120 | loop fusion | flops 42240 | bytes 7016 | tf_op jit(solution)/shard_map/eq | solution.py:206
  302.3 30.3 %multiply_convert_fusion.1 = (bf16[768,3072]{1,0:T(8,128)(2,1)S(1)}, f32[768,3072]{1,0:T(8,128)}, f32[768,3072]{1,0:T(8,128)}) fusion(f32[3072]{0:T(1024)S(1)} %copy-done.38, bf16[768,3072]{1,0:T(8,128)(2,1)} %param.35, f32[768,768]{0,1:T(8,128)S(1)} %get-tuple-element.372, f32[768]{0:T(1024)S(1)} %copy-done.42, f32[768]{0:T(1024)S(1)} %copy-done.33, ...), kind=kOutput, calls=%fused_computation.57 | convolution fusion | flops 3782541312 | bytes 30695424 | tf_op jit(solution)/shard_map/dot_general | solution.py:195
  358.8 15.4 %convert_reduce_fusion = (f32[3072]{0:T(1024)}, bf16[768,3072]{1,0:T(8,128)(2,1)}) fusion(f32[768,3072]{1,0:T(8,128)} %get-tuple-element.341, bf16[3072,768]{1,0:T(8,128)(2,1)} %param.37, f32[768,768]{0,1:T(8,128)S(1)} %get-tuple-element.334, f32[768,3072]{1,0:T(8,128)} %get-tuple-element.373, f32[3072]{0:T(1024)S(1)} %copy-done.39), kind=kOutput, calls=%fused_computation.55 | convolution fusion | flops 3664573440 | bytes 30695424 | tf_op jit(solution)/shard_map/dot_general | solution.py:244
  419.1 22.6 %all-to-all-done.2 = bf16[4,192,768]{2,1,0:T(8,128)(2,1)} async-done(((bf16[4,192,768]{2,1,0:T(8,128)(2,1)}), bf16[4,192,768]{2,1,0:T(8,128)(2,1)}, u32[]{:S(2)}, u32[]{:S(2)}) %all-to-all-start.2) | async-done | bytes 1179680 | tf_op jit(solution)/shard_map/all_to_all | solution.py:262
  453.6 333.4 %while.27 = (s32[]{:T(128)}, f32[3,64,4096]{2,1,0:T(8,128)}, f32[3,64,4096]{2,1,0:T(8,128)}, bf16[6,3,64,512]{3,2,1,0:T(8,128)(2,1)}, s32[6]{0:T(128)S(1)}, /*in...) while((s32[]{:T(128)}, f32[3,64,4096]{2,1,0:T(8,128)}, ...), condition=%wide.region_19.20_spmd, body=%wide.region_17.19_spmd.sunk | while | flops 1544361984 | bytes 113093408 | solution.py:125
  471.1 15.8 %fusion.163 = f32[3,64,4096]{2,1,0:T(8,128)} fusion(f32[3,64,4096]{2,1,0:T(8,128)} %get-tuple-element.577, s32[]{:T(128)S(6)} %select_n.97, f32[3,512,1536]{2,1,0:T(8,128)} %subtract_exponential_fusion.4, f32[3,512,1536]{2,1,0:T(8,128)} %fusion.162, bf16[3,64,3072]{2,1,0:T(8,128)(2,1)} %get-tuple-element.598, s32[]{:T(128)S(6)} %select_n.98), kind=kOutput, calls=%fused_computation.31.clone.1 | convolution fusion | flops 314084352 | bytes 40304648 | tf_op jit(solution)/shard_map/while/body/eval_jaxpr/hqk,hdq->hdk/dot_general | solution.py:103
  487.0 15.5 %fusion.165 = bf16[6,3,64,512]{3,2,1,0:T(8,128)(2,1)} fusion(bf16[6,3,64,512]{3,2,1,0:T(8,128)(2,1)} %get-tuple-element.579, s32[]{:T(128)} %get-tuple-element.576, f32[3,512,1536]{2,1,0:T(8,128)} %subtract_exponential_fusion.4, f32[3,512,1536]{2,1,0:T(8,128)} %fusion.162, bf16[3,64,4096]{2,1,0:T(8,128)(2,1)} %get-tuple-element.601, s32[]{:T(128)S(6)} %select_n.97), kind=kOutput, calls=%fused_computation.34.clone.1 | convolution fusion | flops 313789440 | bytes 38732292 | tf_op jit(solution)/shard_map/while/body/eval_jaxpr/hqk,hdk->hdq/dot_general | solution.py:100
  526.3 15.8 %fusion.163 = f32[3,64,4096]{2,1,0:T(8,128)} fusion(f32[3,64,4096]{2,1,0:T(8,128)} %get-tuple-element.577, s32[]{:T(128)S(6)} %select_n.97, f32[3,512,1536]{2,1,0:T(8,128)} %subtract_exponential_fusion.4, f32[3,512,1536]{2,1,0:T(8,128)} %fusion.162, bf16[3,64,3072]{2,1,0:T(8,128)(2,1)} %get-tuple-element.598, s32[]{:T(128)S(6)} %select_n.98), kind=kOutput, calls=%fused_computation.31.clone.1 | convolution fusion | flops 314084352 | bytes 40304648 | tf_op jit(solution)/shard_map/while/body/eval_jaxpr/hqk,hdq->hdk/dot_general | solution.py:103
  542.1 15.4 %fusion.165 = bf16[6,3,64,512]{3,2,1,0:T(8,128)(2,1)} fusion(bf16[6,3,64,512]{3,2,1,0:T(8,128)(2,1)} %get-tuple-element.579, s32[]{:T(128)} %get-tuple-element.576, f32[3,512,1536]{2,1,0:T(8,128)} %subtract_exponential_fusion.4, f32[3,512,1536]{2,1,0:T(8,128)} %fusion.162, bf16[3,64,4096]{2,1,0:T(8,128)(2,1)} %get-tuple-element.601, s32[]{:T(128)S(6)} %select_n.97), kind=kOutput, calls=%fused_computation.34.clone.1 | convolution fusion | flops 313789440 | bytes 38732292 | tf_op jit(solution)/shard_map/while/body/eval_jaxpr/hqk,hdk->hdq/dot_general | solution.py:100
  581.2 17.1 %fusion.163 = f32[3,64,4096]{2,1,0:T(8,128)} fusion(f32[3,64,4096]{2,1,0:T(8,128)} %get-tuple-element.577, s32[]{:T(128)S(6)} %select_n.97, f32[3,512,1536]{2,1,0:T(8,128)} %subtract_exponential_fusion.4, f32[3,512,1536]{2,1,0:T(8,128)} %fusion.162, bf16[3,64,3072]{2,1,0:T(8,128)(2,1)} %get-tuple-element.598, s32[]{:T(128)S(6)} %select_n.98), kind=kOutput, calls=%fused_computation.31.clone.1 | convolution fusion | flops 314084352 | bytes 40304648 | tf_op jit(solution)/shard_map/while/body/eval_jaxpr/hqk,hdq->hdk/dot_general | solution.py:103
  598.3 16.7 %fusion.165 = bf16[6,3,64,512]{3,2,1,0:T(8,128)(2,1)} fusion(bf16[6,3,64,512]{3,2,1,0:T(8,128)(2,1)} %get-tuple-element.579, s32[]{:T(128)} %get-tuple-element.576, f32[3,512,1536]{2,1,0:T(8,128)} %subtract_exponential_fusion.4, f32[3,512,1536]{2,1,0:T(8,128)} %fusion.162, bf16[3,64,4096]{2,1,0:T(8,128)(2,1)} %get-tuple-element.601, s32[]{:T(128)S(6)} %select_n.97), kind=kOutput, calls=%fused_computation.34.clone.1 | convolution fusion | flops 313789440 | bytes 38732292 | tf_op jit(solution)/shard_map/while/body/eval_jaxpr/hqk,hdk->hdq/dot_general | solution.py:100
  638.7 16.1 %fusion.163 = f32[3,64,4096]{2,1,0:T(8,128)} fusion(f32[3,64,4096]{2,1,0:T(8,128)} %get-tuple-element.577, s32[]{:T(128)S(6)} %select_n.97, f32[3,512,1536]{2,1,0:T(8,128)} %subtract_exponential_fusion.4, f32[3,512,1536]{2,1,0:T(8,128)} %fusion.162, bf16[3,64,3072]{2,1,0:T(8,128)(2,1)} %get-tuple-element.598, s32[]{:T(128)S(6)} %select_n.98), kind=kOutput, calls=%fused_computation.31.clone.1 | convolution fusion | flops 314084352 | bytes 40304648 | tf_op jit(solution)/shard_map/while/body/eval_jaxpr/hqk,hdq->hdk/dot_general | solution.py:103
  654.8 15.4 %fusion.165 = bf16[6,3,64,512]{3,2,1,0:T(8,128)(2,1)} fusion(bf16[6,3,64,512]{3,2,1,0:T(8,128)(2,1)} %get-tuple-element.579, s32[]{:T(128)} %get-tuple-element.576, f32[3,512,1536]{2,1,0:T(8,128)} %subtract_exponential_fusion.4, f32[3,512,1536]{2,1,0:T(8,128)} %fusion.162, bf16[3,64,4096]{2,1,0:T(8,128)(2,1)} %get-tuple-element.601, s32[]{:T(128)S(6)} %select_n.97), kind=kOutput, calls=%fused_computation.34.clone.1 | convolution fusion | flops 313789440 | bytes 38732292 | tf_op jit(solution)/shard_map/while/body/eval_jaxpr/hqk,hdk->hdq/dot_general | solution.py:100
  693.9 15.8 %fusion.163 = f32[3,64,4096]{2,1,0:T(8,128)} fusion(f32[3,64,4096]{2,1,0:T(8,128)} %get-tuple-element.577, s32[]{:T(128)S(6)} %select_n.97, f32[3,512,1536]{2,1,0:T(8,128)} %subtract_exponential_fusion.4, f32[3,512,1536]{2,1,0:T(8,128)} %fusion.162, bf16[3,64,3072]{2,1,0:T(8,128)(2,1)} %get-tuple-element.598, s32[]{:T(128)S(6)} %select_n.98), kind=kOutput, calls=%fused_computation.31.clone.1 | convolution fusion | flops 314084352 | bytes 40304648 | tf_op jit(solution)/shard_map/while/body/eval_jaxpr/hqk,hdq->hdk/dot_general | solution.py:103
  709.7 15.7 %fusion.165 = bf16[6,3,64,512]{3,2,1,0:T(8,128)(2,1)} fusion(bf16[6,3,64,512]{3,2,1,0:T(8,128)(2,1)} %get-tuple-element.579, s32[]{:T(128)} %get-tuple-element.576, f32[3,512,1536]{2,1,0:T(8,128)} %subtract_exponential_fusion.4, f32[3,512,1536]{2,1,0:T(8,128)} %fusion.162, bf16[3,64,4096]{2,1,0:T(8,128)(2,1)} %get-tuple-element.601, s32[]{:T(128)S(6)} %select_n.97), kind=kOutput, calls=%fused_computation.34.clone.1 | convolution fusion | flops 313789440 | bytes 38732292 | tf_op jit(solution)/shard_map/while/body/eval_jaxpr/hqk,hdk->hdq/dot_general | solution.py:100
  749.6 15.9 %fusion.163 = f32[3,64,4096]{2,1,0:T(8,128)} fusion(f32[3,64,4096]{2,1,0:T(8,128)} %get-tuple-element.577, s32[]{:T(128)S(6)} %select_n.97, f32[3,512,1536]{2,1,0:T(8,128)} %subtract_exponential_fusion.4, f32[3,512,1536]{2,1,0:T(8,128)} %fusion.162, bf16[3,64,3072]{2,1,0:T(8,128)(2,1)} %get-tuple-element.598, s32[]{:T(128)S(6)} %select_n.98), kind=kOutput, calls=%fused_computation.31.clone.1 | convolution fusion | flops 314084352 | bytes 40304648 | tf_op jit(solution)/shard_map/while/body/eval_jaxpr/hqk,hdq->hdk/dot_general | solution.py:103
  765.4 15.4 %fusion.165 = bf16[6,3,64,512]{3,2,1,0:T(8,128)(2,1)} fusion(bf16[6,3,64,512]{3,2,1,0:T(8,128)(2,1)} %get-tuple-element.579, s32[]{:T(128)} %get-tuple-element.576, f32[3,512,1536]{2,1,0:T(8,128)} %subtract_exponential_fusion.4, f32[3,512,1536]{2,1,0:T(8,128)} %fusion.162, bf16[3,64,4096]{2,1,0:T(8,128)(2,1)} %get-tuple-element.601, s32[]{:T(128)S(6)} %select_n.97), kind=kOutput, calls=%fused_computation.34.clone.1 | convolution fusion | flops 313789440 | bytes 38732292 | tf_op jit(solution)/shard_map/while/body/eval_jaxpr/hqk,hdk->hdq/dot_general | solution.py:100
  809.9 157.8 %all_to_all.62 = bf16[3,192,3072]{1,0,2:T(4,128)(2,1)} all-to-all(bf16[3,192,3072]{1,0,2:T(4,128)(2,1)} %copy.165), channel_id=1, replica_groups=mesh['seq'=8,'head'=4] {'head'}, dimensions={2} | all-to-all | bytes 7077888 | tf_op jit(solution)/shard_map/all_to_all | solution.py:275
  997.9 10.8 copy.177
  1017.9 41.1 %all-reduce.14 = (f32[768]{0:T(1024)}, f32[768]{0:T(1024)}, f32[768]{0:T(1024)}, f32[768]{0:T(1024)}, f32[768]{0:T(1024)}, /*index=5*/f32[3072]{0:T(1024)}, f32[...) all-reduce(f32[768]{0:T(1024)} %reduce_sum.241, ...), channel_id=3, replica_groups=mesh['seq'=8,'head'=4] {'seq','head'}, use_global_device_ids=true, to_apply=%region_22.23.clone | all-reduce | flops 12289 | bytes 98312
  1083.2 29.1 %reduce-scatter.17.cloned.1.call-done = f32[24,2304]{1,0:T(8,128)} async-done(((f32[768,2304]{1,0:T(8,128)}), f32[24,2304]{1,0:T(8,128)}) %reduce-scatter.17.cloned.1.call-update) | async-done | bytes 221200
  (338 shorter events, 468.1 us)
Async XLA Ops:
  19.5 111.4 %all-to-all-start = ((bf16[3,768,768]{2,0,1:T(4,128)(2,1)}), bf16[3,768,768]{2,0,1:T(4,128)(2,1)}, u32[]{:S(2)}, u32[]{:S(2)}) async-start(bf16[3,768,768]{2,0,1:T(4,128)(2,1)} %copy.152), calls=%async_computation | async-start | bytes 9437184 | tf_op jit(solution)/shard_map/all_to_all | solution.py:179
  266.0 32.5 %copy-start.40 = (f32[768]{0:T(1024)S(1)}, f32[768]{0:T(1024)}, u32[]{:S(2)}) copy-start(f32[768]{0:T(1024)} %param.32) | copy-start | bytes 9220
  266.0 32.5 %all-to-all-start.1 = ((bf16[192,4,768]{2,0,1:T(8,128)(2,1)}), bf16[192,4,768]{2,0,1:T(8,128)(2,1)}, u32[]{:S(2)}, u32[]{:S(2)}) async-start(bf16[192,4,768]{2,0,1:T(8,128)(2,1)} %copy.158), calls=%async_computation.1 | async-start | bytes 2359296 | tf_op jit(solution)/shard_map/all_to_all | solution.py:184
  270.4 812.8 %reduce-scatter.15.cloned.1.call-start = ((), (), s32[]{:S(2)}) async-start(), calls=%async_computation.12 | async-start | bytes 2433024 | tf_op jit(solution)/shard_map/reduce_scatter | solution.py:300
  275.2 18.6 %copy-start.19 = (s32[768]{0:T(1024)}, s32[768]{0:T(1024)S(1)}, u32[]{:S(2)}) copy-start(s32[768]{0:T(1024)S(1)} %iota_add_fusion) | copy-start | bytes 9220
  298.5 34.1 %slice-start = ((s8[4718592]{0:T(1024)(128)(4,1)}), s8[4194304]{0:T(1024)(128)(4,1)S(1)}, s32[]{:S(2)}) async-start(s8[4718592]{0:T(1024)(128)(4,1)} %bitcast.131), calls=%async_computation.14 | async-start | bytes 8388608
  301.9 30.7 %copy-start.5 = (f32[768,768]{0,1:T(8,128)}, f32[768,768]{0,1:T(8,128)S(1)}, u32[]{:S(2)}) copy-start(f32[768,768]{0,1:T(8,128)S(1)} %get-tuple-element.372) | copy-start | bytes 7077892
  301.9 30.7 %copy-start.17 = (f32[768]{0:T(1024)}, f32[768]{0:T(1024)S(1)}, u32[]{:S(2)}) copy-start(f32[768]{0:T(1024)S(1)} %broadcast_multiply_fusion.5) | copy-start | bytes 9220
  302.2 30.3 %copy-start.24 = (f32[768]{0:T(1024)}, f32[768]{0:T(1024)S(1)}, u32[]{:S(2)}) copy-start(f32[768]{0:T(1024)S(1)} %add_rsqrt_fusion.1) | copy-start | bytes 9220
  302.2 30.3 %slice-start.1 = ((s8[4718592]{0:T(1024)(128)(4,1)}), s8[524288]{0:T(1024)(128)(4,1)S(1)}, s32[]{:S(2)}) async-start(s8[4718592]{0:T(1024)(128)(4,1)} %bitcast.131), calls=%async_computation.15 | async-start | bytes 1048576
  302.2 30.3 %copy-start.41 = (f32[768]{0:T(1024)S(1)}, f32[768]{0:T(1024)}, u32[]{:S(2)}) copy-start(f32[768]{0:T(1024)} %param.38) | copy-start | bytes 9220
  352.6 730.6 %reduce-scatter.9.cloned.1.call-start = ((), (), s32[]{:S(2)}) async-start(), calls=%async_computation.9 | async-start | bytes 2433024 | tf_op jit(solution)/shard_map/reduce_scatter | solution.py:290
  357.3 16.9 %slice-start.2 = ((s8[4718592]{0:T(1024)(128)(4,1)}), s8[4194304]{0:T(1024)(128)(4,1)S(1)}, s32[]{:S(2)}) async-start(s8[4718592]{0:T(1024)(128)(4,1)} %bitcast.133), calls=%async_computation.16 | async-start | bytes 8388608
  358.8 15.5 %copy-start.10 = (f32[768,768]{0,1:T(8,128)}, f32[768,768]{0,1:T(8,128)S(1)}, u32[]{:S(2)}) copy-start(f32[768,768]{0,1:T(8,128)S(1)} %get-tuple-element.334) | copy-start | bytes 7077892
  358.8 15.5 %copy-start.6 = (f32[768,768]{0,1:T(8,128)S(1)}, f32[768,768]{0,1:T(8,128)}, u32[]{:S(2)}) copy-start(f32[768,768]{0,1:T(8,128)} %copy-done.5) | copy-start | bytes 7077892
  358.8 15.5 %copy-start.18 = (f32[768]{0:T(1024)S(1)}, f32[768]{0:T(1024)}, u32[]{:S(2)}) copy-start(f32[768]{0:T(1024)} %copy-done.17) | copy-start | bytes 9220
  358.8 15.5 %copy-start.25 = (f32[768]{0:T(1024)S(1)}, f32[768]{0:T(1024)}, u32[]{:S(2)}) copy-start(f32[768]{0:T(1024)} %copy-done.24) | copy-start | bytes 9220
  358.8 15.5 %copy-start.34 = (f32[768]{0:T(1024)S(1)}, f32[768]{0:T(1024)}, u32[]{:S(2)}) copy-start(f32[768]{0:T(1024)} %param.33) | copy-start | bytes 9220
  358.8 15.5 %slice-start.3 = ((s8[4718592]{0:T(1024)(128)(4,1)}), s8[524288]{0:T(1024)(128)(4,1)S(1)}, s32[]{:S(2)}) async-start(s8[4718592]{0:T(1024)(128)(4,1)} %bitcast.133), calls=%async_computation.17 | async-start | bytes 1048576
  388.6 694.6 %reduce-scatter.11.cloned.1.call-start = ((), (), s32[]{:S(2)}) async-start(), calls=%async_computation.10 | async-start | bytes 9732096 | tf_op jit(solution)/shard_map/reduce_scatter | solution.py:294
  403.9 37.8 %all-to-all-start.2 = ((bf16[4,192,768]{2,1,0:T(8,128)(2,1)}), bf16[4,192,768]{2,1,0:T(8,128)(2,1)}, u32[]{:S(2)}, u32[]{:S(2)}) async-start(bf16[4,192,768]{2,1,0:T(8,128)(2,1)} %bitcast.127), calls=%async_computation.2 | async-start | bytes 2359296 | tf_op jit(solution)/shard_map/all_to_all | solution.py:262
  408.2 675.0 %reduce-scatter.13.cloned.1.call-start = ((), (), s32[]{:S(2)}) async-start(), calls=%async_computation.11 | async-start | bytes 9732096 | tf_op jit(solution)/shard_map/reduce_scatter | solution.py:296
  419.0 693.2 %reduce-scatter.17.cloned.1.call-start = ((), (), s32[]{:S(2)}) async-start(), calls=%async_computation.13 | async-start | bytes 7299072
  997.9 20.0 %copy-start.23 = (f32[768]{0:T(1024)S(1)}, f32[768]{0:T(1024)}, u32[]{:S(2)}) copy-start(f32[768]{0:T(1024)} %get-tuple-element.269) | copy-start | bytes 9220
  (45 other events, 131.7 us)
Sparse Core Ops, SparseCore 0:
  352.7 107.4 reduce-scatter.14
  466.0 98.6 reduce-scatter.8
  571.2 135.1 reduce-scatter.10
  712.7 149.2 reduce-scatter.12
  993.8 118.3 reduce-scatter.16
where the time goes:
time: 1130 us; the launch traced here: 1120 us
  matrix products  474 us (42%)
  blocking collectives  199 us (18%)
  local copies, waits for them, and re-layouts  187 us (17%)
  waiting for transfers between devices  157 us (14%)
  other arithmetic  62.6 us (6%)
  between operations  16.5 us (1%)
  starting transfers between devices  15.9 us (1%)
    all_to_all x1, blocking collectives, local(): lax.all_to_all(grad_stack, 'head', split_axis=2, concat_axis=1, tiled=True)  158 us
    all_to_all x1, waiting for transfers between devices, local(): lax.all_to_all(qkv_low, 'head', split_axis=1, concat_axis=2, tiled=True)  102 us
    dot_general x6, matrix products, one_block(): jnp.einsum('hqk,hdq->hdk', grad_scores, q_block, preferred_element_type=j...  96.5 us
    dot_general x6, matrix products, one_block(): jnp.einsum('hqk,hdk->hdq', grad_scores, k_window, preferred_element_type=...  94.1 us
    dot_general x12, matrix products, block_scores(): jnp.einsum('hdq,hdk->hqk', q_block, k_window, preferred_element_type=jnp....  63.4 us
    unnamed x1, blocking collectives  41.1 us
    dot_general x6, matrix products, one_block(): jnp.einsum('hdq,hdk->hqk', grad_block, v_window, preferred_element_type=j...  37.6 us
    dot_general x6, matrix products, one_block(): jnp.einsum('hqk,hdq->hdk', weights_low, grad_block, preferred_element_typ...  37 us
  transfers between devices with their start and end apart: 8, of which 4 were waited for; matrix products, arithmetic and copies ran while one was open for 47% of the time, Pallas kernels for 0%

commit v1 on v0

--- a/solution.py
+++ b/solution.py
@@ -259,8 +259,14 @@
     grad_ctx_cols = lax.dot_general(
         w_out, grad_attn, contract_last, preferred_element_type=jnp.float32
     )
-    grad_ctx_heads = lax.all_to_all(
-        grad_ctx_cols.astype(jnp.bfloat16), "head", split_axis=0, concat_axis=1, tiled=True
+    grad_ctx_heads = jnp.concatenate(
+        lax.all_to_all(
+            jnp.stack(jnp.split(grad_ctx_cols.astype(jnp.bfloat16), lax.axis_size("head"), axis=0)),
+            "head",
+            0,
+            0,
+        ),
+        axis=1,
     )
     grad_q, grad_k, grad_v = attend_backward(
         q_heads,

time: 1130 us -> 1130 us (level)
    unnamed x114 -> x118, local copies, waits for them, and re-layouts: 36.9 us -> 39.3 us
where the time goes in v1:
time: 1130 us; the launch traced here: 1120 us
  matrix products  471 us (42%)
  blocking collectives  199 us (18%)
  local copies, waits for them, and re-layouts  190 us (17%)
  waiting for transfers between devices  156 us (14%)
  other arithmetic  63.8 us (6%)
  between operations  16.4 us (1%)
  starting transfers between devices  15.8 us (1%)
    all_to_all x1, blocking collectives, local(): lax.all_to_all(grad_stack, 'head', split_axis=2, concat_axis=1, tiled=True)  158 us
    all_to_all x1, waiting for transfers between devices, local(): lax.all_to_all(qkv_low, 'head', split_axis=1, concat_axis=2, tiled=True)  102 us
    dot_general x6, matrix products, one_block(): jnp.einsum('hqk,hdq->hdk', grad_scores, q_block, preferred_element_type=j...  96.5 us
    dot_general x6, matrix products, one_block(): jnp.einsum('hqk,hdk->hdq', grad_scores, k_window, preferred_element_type=...  94.1 us
    dot_general x12, matrix products, block_scores(): jnp.einsum('hdq,hdk->hqk', q_block, k_window, preferred_element_type=jnp....  63.4 us
    unnamed x1, blocking collectives  41.1 us
    unnamed x118, local copies, waits for them, and re-layouts  39.3 us
    dot_general x6, matrix products, one_block(): jnp.einsum('hdq,hdk->hqk', grad_block, v_window, preferred_element_type=j...  37.6 us
  transfers between devices with their start and end apart: 8, of which 4 were waited for; matrix products, arithmetic and copies ran while one was open for 47% of the time, Pallas kernels for 0%

profile of v1, /device:TPU:0, one launch (start us, length us, event | category | flops | bytes accessed | tf_op | source)
XLA Modules:
  0.0 1120.0 jit_solution(7994036309650244012)
XLA Ops:
  29.1 101.8 %all-to-all-done = bf16[3,768,768]{2,0,1:T(4,128)(2,1)} async-done(((bf16[3,768,768]{2,0,1:T(4,128)(2,1)}), bf16[3,768,768]{2,0,1:T(4,128)(2,1)}, u32[]{:S(2)}, u32[]{:S(2)}) %all-to-all-start) | async-done | bytes 3538976 | tf_op jit(solution)/shard_map/all_to_all | solution.py:179
  130.9 11.1 fusion.93
  167.8 88.9 %while.26 = (s32[]{:T(128)}, bf16[6,3,64,512]{3,2,1,0:T(8,128)(2,1)}, f32[6,3,512]{2,1,0:T(4,128)}, s32[6]{0:T(128)S(1)}, bf16[3,64,4096]{2,1,0:T(8,128)(2,1)}, ...) while((s32[]{:T(128)}, ...), condition=%wide.region_5.6_spmd, body=%wide.region_2.5_spmd.sunk | while | flops 633076224 | bytes 33304036 | solution.py:69
  276.4 16.7 %fusion.72 = (pred[768]{0:T(1024)(128)(4,1)}, s32[768]{0:T(1024)S(1)}) fusion(s32[]{:T(128)} %bitcast.16, s32[]{:T(128)} %bitcast.17, s32[]{:T(128)} %bitcast.18, s32[]{:T(128)} %bitcast.19, s32[]{:T(128)} %bitcast.20, s32[]{:T(128)} %bitcast.21, s32[]{:T(128)} %bitcast.22, s32[]{:T(128)} %bitcast.23, s32[]{:T(128)} %bitcast.24, s32[]{:T(128)} %bitcast.25, ...), kind=kLoop, calls=%fused_computation.126 | loop fusion | flops 42240 | bytes 7016 | tf_op jit(solution)/shard_map/eq | solution.py:206
  303.5 28.5 %multiply_convert_fusion.1 = (bf16[768,3072]{1,0:T(8,128)(2,1)S(1)}, f32[768,3072]{1,0:T(8,128)}, f32[768,3072]{1,0:T(8,128)}) fusion(f32[3072]{0:T(1024)S(1)} %copy-done.38, bf16[768,3072]{1,0:T(8,128)(2,1)S(1)} %bitcast.140, f32[768,768]{0,1:T(8,128)S(1)} %get-tuple-element.376, f32[768]{0:T(1024)S(1)} %copy-done.42, f32[768]{0:T(1024)S(1)} %copy-done.33, ...), kind=kOutput, calls=%fused_computation.57 | convolution fusion | flops 3782541312 | bytes 30695424 | tf_op jit(solution)/shard_map/dot_general | solution.py:195
  358.9 15.4 %convert_reduce_fusion = (f32[3072]{0:T(1024)}, bf16[768,3072]{1,0:T(8,128)(2,1)}) fusion(f32[768,3072]{1,0:T(8,128)} %get-tuple-element.341, bf16[3072,768]{1,0:T(8,128)(2,1)} %param.37, f32[768,768]{0,1:T(8,128)S(1)} %get-tuple-element.334, f32[768,3072]{1,0:T(8,128)} %get-tuple-element.377, f32[3072]{0:T(1024)S(1)} %copy-done.39), kind=kOutput, calls=%fused_computation.55 | convolution fusion | flops 3664573440 | bytes 30695424 | tf_op jit(solution)/shard_map/dot_general | solution.py:244
  419.6 21.9 %all-to-all-done.2 = bf16[4,192,768]{2,1,0:T(8,128)(2,1)} async-done(((bf16[4,192,768]{2,1,0:T(8,128)(2,1)}), bf16[4,192,768]{2,1,0:T(8,128)(2,1)}, u32[]{:S(2)}, u32[]{:S(2)}) %all-to-all-start.2) | async-done | bytes 1179680 | tf_op jit(solution)/shard_map/all_to_all | solution.py:263
  453.3 333.5 %while.27 = (s32[]{:T(128)}, f32[3,64,4096]{2,1,0:T(8,128)}, f32[3,64,4096]{2,1,0:T(8,128)}, bf16[6,3,64,512]{3,2,1,0:T(8,128)(2,1)}, s32[6]{0:T(128)S(1)}, /*in...) while((s32[]{:T(128)}, f32[3,64,4096]{2,1,0:T(8,128)}, ...), condition=%wide.region_19.20_spmd, body=%wide.region_17.19_spmd.sunk | while | flops 1544361984 | bytes 113093408 | solution.py:125
  470.9 15.8 %fusion.164 = f32[3,64,4096]{2,1,0:T(8,128)} fusion(f32[3,64,4096]{2,1,0:T(8,128)} %get-tuple-element.581, s32[]{:T(128)S(6)} %select_n.97, f32[3,512,1536]{2,1,0:T(8,128)} %subtract_exponential_fusion.4, f32[3,512,1536]{2,1,0:T(8,128)} %fusion.163, bf16[3,64,3072]{2,1,0:T(8,128)(2,1)} %get-tuple-element.602, s32[]{:T(128)S(6)} %select_n.98), kind=kOutput, calls=%fused_computation.31.clone.1 | convolution fusion | flops 314084352 | bytes 40304648 | tf_op jit(solution)/shard_map/while/body/eval_jaxpr/hqk,hdq->hdk/dot_general | solution.py:103
  486.8 15.5 %fusion.166 = bf16[6,3,64,512]{3,2,1,0:T(8,128)(2,1)} fusion(bf16[6,3,64,512]{3,2,1,0:T(8,128)(2,1)} %get-tuple-element.583, s32[]{:T(128)} %get-tuple-element.580, f32[3,512,1536]{2,1,0:T(8,128)} %subtract_exponential_fusion.4, f32[3,512,1536]{2,1,0:T(8,128)} %fusion.163, bf16[3,64,4096]{2,1,0:T(8,128)(2,1)} %get-tuple-element.605, s32[]{:T(128)S(6)} %select_n.97), kind=kOutput, calls=%fused_computation.34.clone.1 | convolution fusion | flops 313789440 | bytes 38732292 | tf_op jit(solution)/shard_map/while/body/eval_jaxpr/hqk,hdk->hdq/dot_general | solution.py:100
  526.1 15.8 %fusion.164 = f32[3,64,4096]{2,1,0:T(8,128)} fusion(f32[3,64,4096]{2,1,0:T(8,128)} %get-tuple-element.581, s32[]{:T(128)S(6)} %select_n.97, f32[3,512,1536]{2,1,0:T(8,128)} %subtract_exponential_fusion.4, f32[3,512,1536]{2,1,0:T(8,128)} %fusion.163, bf16[3,64,3072]{2,1,0:T(8,128)(2,1)} %get-tuple-element.602, s32[]{:T(128)S(6)} %select_n.98), kind=kOutput, calls=%fused_computation.31.clone.1 | convolution fusion | flops 314084352 | bytes 40304648 | tf_op jit(solution)/shard_map/while/body/eval_jaxpr/hqk,hdq->hdk/dot_general | solution.py:103
  541.9 15.4 %fusion.166 = bf16[6,3,64,512]{3,2,1,0:T(8,128)(2,1)} fusion(bf16[6,3,64,512]{3,2,1,0:T(8,128)(2,1)} %get-tuple-element.583, s32[]{:T(128)} %get-tuple-element.580, f32[3,512,1536]{2,1,0:T(8,128)} %subtract_exponential_fusion.4, f32[3,512,1536]{2,1,0:T(8,128)} %fusion.163, bf16[3,64,4096]{2,1,0:T(8,128)(2,1)} %get-tuple-element.605, s32[]{:T(128)S(6)} %select_n.97), kind=kOutput, calls=%fused_computation.34.clone.1 | convolution fusion | flops 313789440 | bytes 38732292 | tf_op jit(solution)/shard_map/while/body/eval_jaxpr/hqk,hdk->hdq/dot_general | solution.py:100
  581.0 17.1 %fusion.164 = f32[3,64,4096]{2,1,0:T(8,128)} fusion(f32[3,64,4096]{2,1,0:T(8,128)} %get-tuple-element.581, s32[]{:T(128)S(6)} %select_n.97, f32[3,512,1536]{2,1,0:T(8,128)} %subtract_exponential_fusion.4, f32[3,512,1536]{2,1,0:T(8,128)} %fusion.163, bf16[3,64,3072]{2,1,0:T(8,128)(2,1)} %get-tuple-element.602, s32[]{:T(128)S(6)} %select_n.98), kind=kOutput, calls=%fused_computation.31.clone.1 | convolution fusion | flops 314084352 | bytes 40304648 | tf_op jit(solution)/shard_map/while/body/eval_jaxpr/hqk,hdq->hdk/dot_general | solution.py:103
  598.1 16.7 %fusion.166 = bf16[6,3,64,512]{3,2,1,0:T(8,128)(2,1)} fusion(bf16[6,3,64,512]{3,2,1,0:T(8,128)(2,1)} %get-tuple-element.583, s32[]{:T(128)} %get-tuple-element.580, f32[3,512,1536]{2,1,0:T(8,128)} %subtract_exponential_fusion.4, f32[3,512,1536]{2,1,0:T(8,128)} %fusion.163, bf16[3,64,4096]{2,1,0:T(8,128)(2,1)} %get-tuple-element.605, s32[]{:T(128)S(6)} %select_n.97), kind=kOutput, calls=%fused_computation.34.clone.1 | convolution fusion | flops 313789440 | bytes 38732292 | tf_op jit(solution)/shard_map/while/body/eval_jaxpr/hqk,hdk->hdq/dot_general | solution.py:100
  638.5 16.1 %fusion.164 = f32[3,64,4096]{2,1,0:T(8,128)} fusion(f32[3,64,4096]{2,1,0:T(8,128)} %get-tuple-element.581, s32[]{:T(128)S(6)} %select_n.97, f32[3,512,1536]{2,1,0:T(8,128)} %subtract_exponential_fusion.4, f32[3,512,1536]{2,1,0:T(8,128)} %fusion.163, bf16[3,64,3072]{2,1,0:T(8,128)(2,1)} %get-tuple-element.602, s32[]{:T(128)S(6)} %select_n.98), kind=kOutput, calls=%fused_computation.31.clone.1 | convolution fusion | flops 314084352 | bytes 40304648 | tf_op jit(solution)/shard_map/while/body/eval_jaxpr/hqk,hdq->hdk/dot_general | solution.py:103
  654.7 15.4 %fusion.166 = bf16[6,3,64,512]{3,2,1,0:T(8,128)(2,1)} fusion(bf16[6,3,64,512]{3,2,1,0:T(8,128)(2,1)} %get-tuple-element.583, s32[]{:T(128)} %get-tuple-element.580, f32[3,512,1536]{2,1,0:T(8,128)} %subtract_exponential_fusion.4, f32[3,512,1536]{2,1,0:T(8,128)} %fusion.163, bf16[3,64,4096]{2,1,0:T(8,128)(2,1)} %get-tuple-element.605, s32[]{:T(128)S(6)} %select_n.97), kind=kOutput, calls=%fused_computation.34.clone.1 | convolution fusion | flops 313789440 | bytes 38732292 | tf_op jit(solution)/shard_map/while/body/eval_jaxpr/hqk,hdk->hdq/dot_general | solution.py:100
  693.7 15.8 %fusion.164 = f32[3,64,4096]{2,1,0:T(8,128)} fusion(f32[3,64,4096]{2,1,0:T(8,128)} %get-tuple-element.581, s32[]{:T(128)S(6)} %select_n.97, f32[3,512,1536]{2,1,0:T(8,128)} %subtract_exponential_fusion.4, f32[3,512,1536]{2,1,0:T(8,128)} %fusion.163, bf16[3,64,3072]{2,1,0:T(8,128)(2,1)} %get-tuple-element.602, s32[]{:T(128)S(6)} %select_n.98), kind=kOutput, calls=%fused_computation.31.clone.1 | convolution fusion | flops 314084352 | bytes 40304648 | tf_op jit(solution)/shard_map/while/body/eval_jaxpr/hqk,hdq->hdk/dot_general | solution.py:103
  709.5 15.7 %fusion.166 = bf16[6,3,64,512]{3,2,1,0:T(8,128)(2,1)} fusion(bf16[6,3,64,512]{3,2,1,0:T(8,128)(2,1)} %get-tuple-element.583, s32[]{:T(128)} %get-tuple-element.580, f32[3,512,1536]{2,1,0:T(8,128)} %subtract_exponential_fusion.4, f32[3,512,1536]{2,1,0:T(8,128)} %fusion.163, bf16[3,64,4096]{2,1,0:T(8,128)(2,1)} %get-tuple-element.605, s32[]{:T(128)S(6)} %select_n.97), kind=kOutput, calls=%fused_computation.34.clone.1 | convolution fusion | flops 313789440 | bytes 38732292 | tf_op jit(solution)/shard_map/while/body/eval_jaxpr/hqk,hdk->hdq/dot_general | solution.py:100
  749.4 15.8 %fusion.164 = f32[3,64,4096]{2,1,0:T(8,128)} fusion(f32[3,64,4096]{2,1,0:T(8,128)} %get-tuple-element.581, s32[]{:T(128)S(6)} %select_n.97, f32[3,512,1536]{2,1,0:T(8,128)} %subtract_exponential_fusion.4, f32[3,512,1536]{2,1,0:T(8,128)} %fusion.163, bf16[3,64,3072]{2,1,0:T(8,128)(2,1)} %get-tuple-element.602, s32[]{:T(128)S(6)} %select_n.98), kind=kOutput, calls=%fused_computation.31.clone.1 | convolution fusion | flops 314084352 | bytes 40304648 | tf_op jit(solution)/shard_map/while/body/eval_jaxpr/hqk,hdq->hdk/dot_general | solution.py:103
  765.3 15.4 %fusion.166 = bf16[6,3,64,512]{3,2,1,0:T(8,128)(2,1)} fusion(bf16[6,3,64,512]{3,2,1,0:T(8,128)(2,1)} %get-tuple-element.583, s32[]{:T(128)} %get-tuple-element.580, f32[3,512,1536]{2,1,0:T(8,128)} %subtract_exponential_fusion.4, f32[3,512,1536]{2,1,0:T(8,128)} %fusion.163, bf16[3,64,4096]{2,1,0:T(8,128)(2,1)} %get-tuple-element.605, s32[]{:T(128)S(6)} %select_n.97), kind=kOutput, calls=%fused_computation.34.clone.1 | convolution fusion | flops 313789440 | bytes 38732292 | tf_op jit(solution)/shard_map/while/body/eval_jaxpr/hqk,hdk->hdq/dot_general | solution.py:100
  809.7 157.8 %all_to_all.51 = bf16[3,192,3072]{1,0,2:T(4,128)(2,1)} all-to-all(bf16[3,192,3072]{1,0,2:T(4,128)(2,1)} %copy.164), channel_id=1, replica_groups=mesh['seq'=8,'head'=4] {'head'}, dimensions={2} | all-to-all | bytes 7077888 | tf_op jit(solution)/shard_map/all_to_all | solution.py:281
  997.7 10.8 copy.176
  1017.8 41.1 %all-reduce.14 = (f32[768]{0:T(1024)}, f32[768]{0:T(1024)}, f32[768]{0:T(1024)}, f32[768]{0:T(1024)}, f32[768]{0:T(1024)}, /*index=5*/f32[3072]{0:T(1024)}, f32[...) all-reduce(f32[768]{0:T(1024)} %reduce_sum.241, ...), channel_id=3, replica_groups=mesh['seq'=8,'head'=4] {'seq','head'}, use_global_device_ids=true, to_apply=%region_22.23.clone | all-reduce | flops 12289 | bytes 98312
  1083.0 29.1 %reduce-scatter.17.cloned.1.call-done = f32[24,2304]{1,0:T(8,128)} async-done(((f32[768,2304]{1,0:T(8,128)}), f32[24,2304]{1,0:T(8,128)}) %reduce-scatter.17.cloned.1.call-update) | async-done | bytes 221200
  (345 shorter events, 470.4 us)
Async XLA Ops:
  19.5 111.4 %all-to-all-start = ((bf16[3,768,768]{2,0,1:T(4,128)(2,1)}), bf16[3,768,768]{2,0,1:T(4,128)(2,1)}, u32[]{:S(2)}, u32[]{:S(2)}) async-start(bf16[3,768,768]{2,0,1:T(4,128)(2,1)} %copy.151), calls=%async_computation | async-start | bytes 9437184 | tf_op jit(solution)/shard_map/all_to_all | solution.py:179
  266.0 32.3 %all-to-all-start.1 = ((bf16[192,4,768]{2,0,1:T(8,128)(2,1)}), bf16[192,4,768]{2,0,1:T(8,128)(2,1)}, u32[]{:S(2)}, u32[]{:S(2)}) async-start(bf16[192,4,768]{2,0,1:T(8,128)(2,1)} %copy.157), calls=%async_computation.1 | async-start | bytes 2359296 | tf_op jit(solution)/shard_map/all_to_all | solution.py:184
  270.2 28.1 %copy-start.40 = (f32[768]{0:T(1024)S(1)}, f32[768]{0:T(1024)}, u32[]{:S(2)}) copy-start(f32[768]{0:T(1024)} %param.32) | copy-start | bytes 9220
  270.3 812.8 %reduce-scatter.15.cloned.1.call-start = ((), (), s32[]{:S(2)}) async-start(), calls=%async_computation.12 | async-start | bytes 2433024 | tf_op jit(solution)/shard_map/reduce_scatter | solution.py:306
  275.1 18.6 %copy-start.19 = (s32[768]{0:T(1024)}, s32[768]{0:T(1024)S(1)}, u32[]{:S(2)}) copy-start(s32[768]{0:T(1024)S(1)} %iota_add_fusion) | copy-start | bytes 9220
  298.3 33.7 %slice-start = ((s8[4718592]{0:T(1024)(128)(4,1)}), s8[4194304]{0:T(1024)(128)(4,1)S(1)}, s32[]{:S(2)}) async-start(s8[4718592]{0:T(1024)(128)(4,1)} %bitcast.137), calls=%async_computation.14 | async-start | bytes 8388608
  301.7 30.3 %copy-start.5 = (f32[768,768]{0,1:T(8,128)}, f32[768,768]{0,1:T(8,128)S(1)}, u32[]{:S(2)}) copy-start(f32[768,768]{0,1:T(8,128)S(1)} %get-tuple-element.376) | copy-start | bytes 7077892
  301.8 30.3 %copy-start.17 = (f32[768]{0:T(1024)}, f32[768]{0:T(1024)S(1)}, u32[]{:S(2)}) copy-start(f32[768]{0:T(1024)S(1)} %broadcast_multiply_fusion.5) | copy-start | bytes 9220
  303.5 28.6 %copy-start.24 = (f32[768]{0:T(1024)}, f32[768]{0:T(1024)S(1)}, u32[]{:S(2)}) copy-start(f32[768]{0:T(1024)S(1)} %add_rsqrt_fusion.1) | copy-start | bytes 9220
  303.5 28.6 %slice-start.1 = ((s8[4718592]{0:T(1024)(128)(4,1)}), s8[524288]{0:T(1024)(128)(4,1)S(1)}, s32[]{:S(2)}) async-start(s8[4718592]{0:T(1024)(128)(4,1)} %bitcast.137), calls=%async_computation.15 | async-start | bytes 1048576
  303.5 28.6 %copy-start.41 = (f32[768]{0:T(1024)S(1)}, f32[768]{0:T(1024)}, u32[]{:S(2)}) copy-start(f32[768]{0:T(1024)} %param.38) | copy-start | bytes 9220
  352.1 730.9 %reduce-scatter.9.cloned.1.call-start = ((), (), s32[]{:S(2)}) async-start(), calls=%async_computation.9 | async-start | bytes 2433024 | tf_op jit(solution)/shard_map/reduce_scatter | solution.py:296
  357.4 16.9 %slice-start.4 = ((s8[4718592]{0:T(1024)(128)(4,1)}), s8[4194304]{0:T(1024)(128)(4,1)S(1)}, s32[]{:S(2)}) async-start(s8[4718592]{0:T(1024)(128)(4,1)} %bitcast.141), calls=%async_computation.18 | async-start | bytes 8388608
  358.9 15.4 %copy-start.10 = (f32[768,768]{0,1:T(8,128)}, f32[768,768]{0,1:T(8,128)S(1)}, u32[]{:S(2)}) copy-start(f32[768,768]{0,1:T(8,128)S(1)} %get-tuple-element.334) | copy-start | bytes 7077892
  358.9 15.4 %copy-start.6 = (f32[768,768]{0,1:T(8,128)S(1)}, f32[768,768]{0,1:T(8,128)}, u32[]{:S(2)}) copy-start(f32[768,768]{0,1:T(8,128)} %copy-done.5) | copy-start | bytes 7077892
  358.9 15.4 %copy-start.18 = (f32[768]{0:T(1024)S(1)}, f32[768]{0:T(1024)}, u32[]{:S(2)}) copy-start(f32[768]{0:T(1024)} %copy-done.17) | copy-start | bytes 9220
  358.9 15.4 %copy-start.25 = (f32[768]{0:T(1024)S(1)}, f32[768]{0:T(1024)}, u32[]{:S(2)}) copy-start(f32[768]{0:T(1024)} %copy-done.24) | copy-start | bytes 9220
  358.9 15.4 %copy-start.34 = (f32[768]{0:T(1024)S(1)}, f32[768]{0:T(1024)}, u32[]{:S(2)}) copy-start(f32[768]{0:T(1024)} %param.33) | copy-start | bytes 9220
  358.9 15.4 %slice-start.5 = ((s8[4718592]{0:T(1024)(128)(4,1)}), s8[524288]{0:T(1024)(128)(4,1)S(1)}, s32[]{:S(2)}) async-start(s8[4718592]{0:T(1024)(128)(4,1)} %bitcast.141), calls=%async_computation.19 | async-start | bytes 1048576
  388.6 694.4 %reduce-scatter.11.cloned.1.call-start = ((), (), s32[]{:S(2)}) async-start(), calls=%async_computation.10 | async-start | bytes 9732096 | tf_op jit(solution)/shard_map/reduce_scatter | solution.py:300
  404.3 37.2 %all-to-all-start.2 = ((bf16[4,192,768]{2,1,0:T(8,128)(2,1)}), bf16[4,192,768]{2,1,0:T(8,128)(2,1)}, u32[]{:S(2)}, u32[]{:S(2)}) async-start(bf16[4,192,768]{2,1,0:T(8,128)(2,1)} %pad_maximum_fusion.1), calls=%async_computation.2 | async-start | bytes 2359296 | tf_op jit(solution)/shard_map/all_to_all | solution.py:263
  408.6 674.4 %reduce-scatter.13.cloned.1.call-start = ((), (), s32[]{:S(2)}) async-start(), calls=%async_computation.11 | async-start | bytes 9732096 | tf_op jit(solution)/shard_map/reduce_scatter | solution.py:302
  419.5 692.6 %reduce-scatter.17.cloned.1.call-start = ((), (), s32[]{:S(2)}) async-start(), calls=%async_computation.13 | async-start | bytes 7299072
  1008.5 9.2 copy-start.23
  (47 other events, 115.8 us)
Sparse Core Ops, SparseCore 0:
  352.3 107.5 reduce-scatter.14
  465.7 98.6 reduce-scatter.8
  570.9 135.2 reduce-scatter.10
  712.5 149.1 reduce-scatter.12
  993.6 118.4 reduce-scatter.16
